TPU v7x, 128 devices: a whole 4x4x4 slice. The times are simulated.
128 devices in a mesh: row: 8 (over z, core), col: 16 (over x, y).
Axes of the slice: x: 4, y: 4, z: 4, core: 2. Of those that a mesh axis runs over, the one named last changes fastest.
Arguments:
- embed: bfloat16 [262144, 64], P(('row', 'col')), may hold values from -6 to 6
- tiles: bfloat16 [8192, 128, 128], P(('row', 'col'))
- tile_rows: int32 [8192], P(('row', 'col')), may hold values from 0 to 2047, as said below
- tile_cols: int32 [8192], P(('row', 'col')), may hold values from 0 to 2047, as said below
- chg_tiles: bfloat16 [24576, 128, 128], P(('row', 'col'))
- chg_rows: int32 [24576], P(('row', 'col')), may hold values from 0 to 2047, as said below
- chg_cols: int32 [24576], P(('row', 'col')), may hold values from 0 to 2047, as said below
Outputs:
- embedding: float32 [262144, 64], P(('row', 'col'))
Inputs may be any that keep to these rules, and one draw needn't show every extreme that they name: Tile n lies in the row group of the device that holds it: tile_rows[n] // 256 equals (n // 64) // 16. Tile n lies in the column group of the device that holds it: tile_cols[n] // 128 equals (n // 64) % 16. `chg_rows`: one device's list names each transpose owner at most 3 times; in every draw some owner is named exactly 3 times by every device's list. `chg_cols`: read with chg_rows to give the transpose owner.
All inputs are finite; a program needn't handle non-finite values.
Results may differ from a plain program's by a relative error of at most 0.025.
Values may be sent and summed in bfloat16 or wider, within the bound.
A program may use at most 192 MiB of HBM per device.

v0:
```python
import jax
import jax.numpy as jnp
from jax import lax
from jax.sharding import PartitionSpec as P

ITERS = 3
CAP = 3


def block_terms(own, own_rows, own_cols, taken, taken_rows, taken_cols, blocked, row_blocks):
    own_terms = jnp.einsum(
        "nab,nbk->nak", own, blocked[own_cols], preferred_element_type=jnp.float32
    )
    taken_terms = jnp.einsum(
        "nab,nak->nbk", taken, blocked[taken_cols], preferred_element_type=jnp.float32
    )
    return jax.ops.segment_sum(own_terms, own_rows, row_blocks) + jax.ops.segment_sum(
        taken_terms, taken_rows, row_blocks
    )


def local(embed, tiles, tile_rows, tile_cols, chg_tiles, chg_rows, chg_cols):
    rows_dev, feature_width = embed.shape
    tile_size = tiles.shape[1]
    row_count = lax.axis_size("row")
    col_count = lax.axis_size("col")
    devices = row_count * col_count
    row_blocks = rows_dev * col_count // tile_size
    col_blocks = rows_dev * row_count // tile_size
    sub_rows = rows_dev // devices
    owners = chg_cols // row_blocks * col_count + chg_rows // col_blocks
    position = jnp.arange(owners.shape[0], dtype=jnp.int32)
    earlier = position[None, :] < position[:, None]
    slot_rank = jnp.sum(jnp.logical_and(owners[:, None] == owners[None, :], earlier), axis=1)
    outgoing = (
        jnp.zeros((devices, CAP, tile_size, tile_size), jnp.bfloat16)
        .at[owners, slot_rank]
        .set(chg_tiles)
    )
    placing = jnp.stack([chg_cols % row_blocks, chg_rows % col_blocks], axis=1)
    output_slots = jnp.zeros((devices, CAP, 2), jnp.int32).at[owners, slot_rank].set(placing)
    taken, taken_places = (
        lax.all_to_all(outgoing, ("row", "col"), split_axis=0, concat_axis=0, tiled=True),
        lax.all_to_all(output_slots, ("row", "col"), split_axis=0, concat_axis=0, tiled=True),
    )
    taken = taken.reshape(devices * CAP, tile_size, tile_size)
    taken_places = taken_places.reshape(devices * CAP, 2)
    taken_rows = taken_places[:, 0]
    taken_cols = taken_places[:, 1]
    own_rows = tile_rows % row_blocks
    own_cols = tile_cols % col_blocks
    degree_terms = jax.ops.segment_sum(
        jnp.sum(jnp.abs(tiles), axis=2, dtype=jnp.float32), own_rows, row_blocks
    )
    degree_terms = degree_terms + jax.ops.segment_sum(
        jnp.sum(jnp.abs(taken), axis=1, dtype=jnp.float32), taken_rows, row_blocks
    )
    degree = 1.0 + lax.psum_scatter(
        degree_terms.astype(jnp.bfloat16), "col", scatter_dimension=0, tiled=True
    ).astype(jnp.float32).reshape(rows_dev, 1)
    nodes = rows_dev * devices
    current = embed
    final_output = embed.astype(jnp.float32)
    for iteration in range(ITERS):
        received_terms = lax.all_to_all(
            current.reshape(devices, sub_rows, feature_width),
            ("row", "col"),
            split_axis=0,
            concat_axis=0,
            tiled=True,
        )
        group = lax.all_gather(
            received_terms.reshape(rows_dev, feature_width), "row", axis=0, tiled=True
        )
        blocked = group.reshape(col_blocks, tile_size, feature_width)
        partial_value = block_terms(
            tiles, own_rows, own_cols, taken, taken_rows, taken_cols, blocked, row_blocks
        )
        summed = lax.psum_scatter(
            partial_value.reshape(row_blocks * tile_size, feature_width).astype(jnp.bfloat16),
            "col",
            scatter_dimension=0,
            tiled=True,
        ).astype(jnp.float32)
        scaled = summed / degree
        local_gram = jnp.dot(
            scaled.T, scaled, precision=lax.Precision.HIGHEST, preferred_element_type=jnp.float32
        )
        gram = lax.psum(local_gram, ("row", "col")) / nodes
        lower = jnp.linalg.cholesky(gram)
        final_output = lax.linalg.triangular_solve(
            lower, scaled, left_side=False, lower=True, transpose_a=True
        )
        current = final_output.astype(jnp.bfloat16)
    return final_output


def solution(mesh):
    placed = (
        P(("row", "col"), None),
        P(("row", "col"), None, None),
        P(("row", "col")),
        P(("row", "col")),
        P(("row", "col"), None, None),
        P(("row", "col")),
        P(("row", "col")),
    )
    return jax.shard_map(
        local, mesh=mesh, in_specs=placed, out_specs=P(("row", "col"), None), check_vma=False
    )
```

profile of v0, /device:TPU:1, one launch (start us, length us, event | category | flops | bytes accessed | tf_op | source)
XLA Modules:
  0.0 1204.5 jit_solution(14980614209809009102)
XLA Ops:
  8.4 10.1 scatter_fusion.1
  20.0 11.5 all-to-all-start.1
  53.4 30.8 %scatter_fusion.2 = bf16[128,3,128,128]{3,2,1,0:T(8,128)(2,1)} fusion(bf16[128,3,128,128]{3,2,1,0:T(8,128)(2,1)} %broadcast_in_dim.14, s32[192]{0:T(256)S(1)} %bitcast.91, bf16[192,128,128]{2,1,0:T(8,128)(2,1)} %param.14), kind=kCustom, calls=%fused_computation.8 | custom fusion | bytes 18875904 | tf_op jit(solution)/shard_map/scatter | solution.py:38
  84.2 10.2 all-to-all-start.2
  97.6 142.3 %all-gather.4.cloned.1.call-done = bf16[16384,64]{1,0:T(8,128)(2,1)} async-done(((bf16[2048,64]{1,0:T(8,128)(2,1)}), bf16[16384,64]{1,0:T(8,128)(2,1)}) %all-gather.4.cloned.1.call-update) | async-done | bytes 2097168 | tf_op jit(solution)/shard_map/all_gather | solution.py:72
  243.8 13.3 %gather_fusion.1 = bf16[384,128,64]{1,2,0:T(8,128)(2,1)} fusion(bf16[128,128,64]{1,2,0:T(8,128)(2,1)S(1)} %copy.77, s32[1024]{0:T(1024)S(1)} %pad_clamp_fusion), kind=kCustom, calls=%fused_computation.1 | custom fusion | bytes 12584448 | tf_op jit(solution)/shard_map/gather | solution.py:15
  265.2 9.0 scatter_fusion
  274.2 9.2 convert_reduce_fusion
  286.7 14.3 %fusion.38 = f32[384,128,64]{1,2,0:T(8,128)} fusion(bf16[384,128,64]{1,2,0:T(8,128)(2,1)} %gather_fusion.1, bf16[384,128,128]{2,1,0:T(8,128)(2,1)} %bitcast.9), kind=kOutput, calls=%fused_computation.120 | convolution fusion | flops 805306368 | bytes 31457280 | tf_op jit(solution)/shard_map/nab,nak->nbk/dot_general | solution.py:14
  305.3 59.8 %scatter_fusion.3 = f32[256,128,64]{1,2,0:T(8,128)} fusion(f32[256,128,64]{1,2,0:T(8,128)} %broadcast.110.clone.3, s32[384]{0:T(512)S(1)} %get-tuple-element.8, f32[384,128,64]{1,2,0:T(8,128)} %fusion.38), kind=kCustom, calls=%fused_computation.9 | custom fusion | flops 3145728 | bytes 37750272 | tf_op jit(solution)/shard_map/scatter-add | solution.py:17
  365.1 8.6 copy_bitcast_fusion.2
  375.0 8.3 all-reduce.3.cloned.1.call-done
  384.0 84.0 %reduce-scatter.4.cloned.1.call-done = bf16[2048,64]{0,1:T(8,128)(2,1)} async-done(((bf16[32768,64]{0,1:T(8,128)(2,1)}), bf16[2048,64]{0,1:T(8,128)(2,1)}) %reduce-scatter.4.cloned.1.call-update) | async-done | bytes 262160 | tf_op jit(solution)/shard_map/reduce_scatter | solution.py:79
  469.7 66.1 %psum.21 = f32[64,64]{0,1:T(8,128)S(1)} all-reduce(f32[64,64]{0,1:T(8,128)S(1)} %fusion.5), channel_id=1, replica_groups=mesh['row'=8,'col'=16] {'row','col'}, use_global_device_ids=true, to_apply=%region_11.12 | all-reduce | flops 4096 | bytes 32768 | tf_op jit(solution)/shard_map/psum | solution.py:89
  550.2 15.7 %all_to_all.25 = bf16[128,2,512]{2,1,0:T(2,128)(2,1)S(1)} all-to-all(bf16[128,2,512]{2,1,0:T(2,128)(2,1)S(1)} %reshape.237), channel_id=1, replica_groups=mesh['row'=8,'col'=16] {'row','col'}, dimensions={0} | all-to-all | bytes 524288 | tf_op jit(solution)/shard_map/all_to_all | solution.py:65
  567.3 28.7 %all-gather.6.cloned.1.call-done = bf16[16384,64]{1,0:T(8,128)(2,1)} async-done(((bf16[2048,64]{1,0:T(8,128)(2,1)}), bf16[16384,64]{1,0:T(8,128)(2,1)}) %all-gather.6.cloned.1.call-update) | async-done | bytes 2097168 | tf_op jit(solution)/shard_map/all_gather | solution.py:72
  599.6 13.3 %gather_fusion.3 = bf16[384,128,64]{1,2,0:T(8,128)(2,1)} fusion(bf16[128,128,64]{1,2,0:T(8,128)(2,1)S(1)} %copy.87, s32[1024]{0:T(1024)S(1)} %pad_clamp_fusion), kind=kCustom, calls=%fused_computation.3 | custom fusion | bytes 12584448 | tf_op jit(solution)/shard_map/gather | solution.py:15
  613.7 14.4 %fusion.39 = f32[384,128,64]{1,2,0:T(8,128)} fusion(bf16[384,128,64]{1,2,0:T(8,128)(2,1)} %gather_fusion.3, bf16[384,128,128]{2,1,0:T(8,128)(2,1)} %bitcast.9), kind=kOutput, calls=%fused_computation.121 | convolution fusion | flops 805306368 | bytes 31457280 | tf_op jit(solution)/shard_map/nab,nak->nbk/dot_general | solution.py:14
  633.9 59.8 %scatter_fusion.5 = f32[256,128,64]{1,2,0:T(8,128)} fusion(f32[256,128,64]{1,2,0:T(8,128)} %broadcast.110.clone.4, s32[384]{0:T(512)S(1)} %get-tuple-element.8, f32[384,128,64]{1,2,0:T(8,128)} %fusion.39), kind=kCustom, calls=%fused_computation.13 | custom fusion | flops 3145728 | bytes 37750272 | tf_op jit(solution)/shard_map/scatter-add | solution.py:17
  698.0 9.2 scatter_fusion.4
  707.2 8.6 copy_bitcast_fusion.1
  715.9 75.9 %reduce-scatter.6.cloned.1.call-done = bf16[2048,64]{0,1:T(8,128)(2,1)} async-done(((bf16[32768,64]{0,1:T(8,128)(2,1)}), bf16[2048,64]{0,1:T(8,128)(2,1)}) %reduce-scatter.6.cloned.1.call-update) | async-done | bytes 262160 | tf_op jit(solution)/shard_map/reduce_scatter | solution.py:79
  793.4 66.2 %psum.22 = f32[64,64]{0,1:T(8,128)S(1)} all-reduce(f32[64,64]{0,1:T(8,128)S(1)} %fusion.6), channel_id=1, replica_groups=mesh['row'=8,'col'=16] {'row','col'}, use_global_device_ids=true, to_apply=%region_17.20 | all-reduce | flops 4096 | bytes 32768 | tf_op jit(solution)/shard_map/psum | solution.py:89
  873.9 15.7 %all_to_all.26 = bf16[128,2,512]{2,1,0:T(2,128)(2,1)S(1)} all-to-all(bf16[128,2,512]{2,1,0:T(2,128)(2,1)S(1)} %reshape.239), channel_id=1, replica_groups=mesh['row'=8,'col'=16] {'row','col'}, dimensions={0} | all-to-all | bytes 524288 | tf_op jit(solution)/shard_map/all_to_all | solution.py:65
  890.9 28.8 %all-gather.8.cloned.1.call-done = bf16[16384,64]{1,0:T(8,128)(2,1)} async-done(((bf16[2048,64]{1,0:T(8,128)(2,1)}), bf16[16384,64]{1,0:T(8,128)(2,1)}) %all-gather.8.cloned.1.call-update) | async-done | bytes 2097168 | tf_op jit(solution)/shard_map/all_gather | solution.py:72
  923.4 13.3 %gather_fusion.5 = bf16[384,128,64]{1,2,0:T(8,128)(2,1)} fusion(bf16[128,128,64]{1,2,0:T(8,128)(2,1)S(1)} %copy.94, s32[1024]{0:T(1024)S(1)} %pad_clamp_fusion), kind=kCustom, calls=%fused_computation.5 | custom fusion | bytes 12584448 | tf_op jit(solution)/shard_map/gather | solution.py:15
  937.5 14.4 %fusion.40 = f32[384,128,64]{1,2,0:T(8,128)} fusion(bf16[384,128,64]{1,2,0:T(8,128)(2,1)} %gather_fusion.5, bf16[384,128,128]{2,1,0:T(8,128)(2,1)} %bitcast.9), kind=kOutput, calls=%fused_computation.122 | convolution fusion | flops 805306368 | bytes 31457280 | tf_op jit(solution)/shard_map/nab,nak->nbk/dot_general | solution.py:14
  957.7 58.9 %scatter_fusion.7 = f32[256,128,64]{1,2,0:T(8,128)} fusion(f32[256,128,64]{1,2,0:T(8,128)} %broadcast.110.clone.5, s32[384]{0:T(512)S(1)} %get-tuple-element.8, f32[384,128,64]{1,2,0:T(8,128)} %fusion.40), kind=kCustom, calls=%fused_computation.15 | custom fusion | flops 3145728 | bytes 37750272 | tf_op jit(solution)/shard_map/scatter-add | solution.py:17
  1020.9 9.2 scatter_fusion.6
  1030.1 8.5 copy_bitcast_fusion
  1038.7 75.5 %reduce-scatter.8.cloned.1.call-done = bf16[2048,64]{0,1:T(8,128)(2,1)} async-done(((bf16[32768,64]{0,1:T(8,128)(2,1)}), bf16[2048,64]{0,1:T(8,128)(2,1)}) %reduce-scatter.8.cloned.1.call-update) | async-done | bytes 262160 | tf_op jit(solution)/shard_map/reduce_scatter | solution.py:79
  1115.9 66.3 %psum.23 = f32[64,64]{0,1:T(8,128)S(1)} all-reduce(f32[64,64]{0,1:T(8,128)S(1)} %fusion.7), channel_id=1, replica_groups=mesh['row'=8,'col'=16] {'row','col'}, use_global_device_ids=true, to_apply=%region_21.24 | all-reduce | flops 4096 | bytes 32768 | tf_op jit(solution)/shard_map/psum | solution.py:89
  (106 shorter events, 128.1 us)
Async XLA Ops:
  20.0 21.6 %all-to-all-start.1 = ((s32[128,3,2]{1,2,0:T(2,128)}), s32[128,3,2]{1,2,0:T(2,128)S(1)}, u32[]{:S(2)}, u32[]{:S(2)}) async-start(s32[128,3,2]{1,2,0:T(2,128)} %copy.79), calls=%async_computation.1 | async-start | bytes 262144 | tf_op jit(solution)/shard_map/all_to_all | solution.py:44
  41.6 42.6 %all-to-all-start = ((bf16[128,2,512]{2,1,0:T(2,128)(2,1)}), bf16[128,2,512]{2,1,0:T(2,128)(2,1)S(1)}, u32[]{:S(2)}, u32[]{:S(2)}) async-start(bf16[128,2,512]{2,1,0:T(2,128)(2,1)} %reshape.235), calls=%async_computation | async-start | bytes 524288 | tf_op jit(solution)/shard_map/all_to_all | solution.py:65
  84.2 11.5 copy-start.3
  84.2 11.6 copy-start
  84.2 13.1 %copy-start.4 = (s32[64]{0:T(128)S(1)}, s32[64]{0:T(128)}, u32[]{:S(2)}) copy-start(s32[64]{0:T(128)} %param.13) | copy-start | bytes 772
  84.2 190.0 %all-to-all-start.2 = ((bf16[128,3,128,128]{3,2,1,0:T(8,128)(2,1)}), bf16[128,3,128,128]{3,2,1,0:T(8,128)(2,1)}, u32[]{:S(2)}, u32[]{:S(2)}) async-start(bf16[128,3,128,128]{3,2,1,0:T(8,128)(2,1)} %scatter_fusion.2), calls=%async_computation.2 | async-start | bytes 25165824 | tf_op jit(solution)/shard_map/all_to_all | solution.py:43
  94.5 145.4 %all-gather.4.cloned.1.call-start = ((), (), s32[]{:S(2)}) async-start(), calls=%async_computation.8 | async-start | bytes 4718592 | tf_op jit(solution)/shard_map/all_gather | solution.py:72
  95.7 287.6 %all-reduce.3.cloned.1.call-start = ((), (), s32[]{:S(2)}) async-start(), calls=%async_computation.14 | async-start | bytes 131072
  286.7 181.4 %reduce-scatter.4.cloned.1.call-start = ((), (), s32[]{:S(2)}) async-start(), calls=%async_computation.9 | async-start | bytes 4456448 | tf_op jit(solution)/shard_map/reduce_scatter | solution.py:79
  365.1 8.7 copy-start.5
  373.7 222.2 %all-gather.6.cloned.1.call-start = ((), (), s32[]{:S(2)}) async-start(), calls=%async_computation.10 | async-start | bytes 4718592 | tf_op jit(solution)/shard_map/all_gather | solution.py:72
  567.1 224.7 %reduce-scatter.6.cloned.1.call-start = ((), (), s32[]{:S(2)}) async-start(), calls=%async_computation.11 | async-start | bytes 4456448 | tf_op jit(solution)/shard_map/reduce_scatter | solution.py:79
  613.7 14.4 %copy-start.1 = (bf16[64,128,128]{2,1,0:T(8,128)(2,1)S(1)}, bf16[64,128,128]{2,1,0:T(8,128)(2,1)}, u32[]{:S(2)}) copy-start(bf16[64,128,128]{2,1,0:T(8,128)(2,1)} %param.11) | copy-start | bytes 6291460
  715.8 203.9 %all-gather.8.cloned.1.call-start = ((), (), s32[]{:S(2)}) async-start(), calls=%async_computation.12 | async-start | bytes 4718592 | tf_op jit(solution)/shard_map/all_gather | solution.py:72
  890.8 223.4 %reduce-scatter.8.cloned.1.call-start = ((), (), s32[]{:S(2)}) async-start(), calls=%async_computation.13 | async-start | bytes 4456448 | tf_op jit(solution)/shard_map/reduce_scatter | solution.py:79
  937.5 14.4 %copy-start.2 = (bf16[64,128,128]{2,1,0:T(8,128)(2,1)S(1)}, bf16[64,128,128]{2,1,0:T(8,128)(2,1)}, u32[]{:S(2)}) copy-start(bf16[64,128,128]{2,1,0:T(8,128)(2,1)} %param.11) | copy-start | bytes 6291460
Sparse Core Ops, SparseCore 0:
  97.1 142.6 all-gather.3
  567.2 28.7 all-gather.5
  891.0 28.7 all-gather.7
Sparse Core Ops, SparseCore 1:
  286.7 96.5 all-reduce.2
  386.9 81.1 reduce-scatter.3
  715.9 75.8 reduce-scatter.5
  1038.8 75.4 reduce-scatter.7
where the time goes:
time: 1210 us; the launch traced here: 1200 us
  waiting for transfers between devices  451 us (37%)
  other arithmetic  283 us (23%)
  blocking collectives  230 us (19%)
  local copies, waits for them, and re-layouts  137 us (11%)
  matrix products  59.8 us (5%)
  starting transfers between devices  26.3 us (2%)
  between operations  16.4 us (1%)
    reduce_scatter x3, waiting for transfers between devices, local(): lax.psum_scatter(partial_value.reshape(row_blocks * tile_size, feature_wi...  235 us
    all_gather x3, waiting for transfers between devices, local(): lax.all_gather(received_terms.reshape(rows_dev, feature_width), 'row', ax...  200 us
    psum x3, blocking collectives, local(): gram = lax.psum(local_gram, ('row', 'col')) / nodes  199 us
    scatter-add x3, other arithmetic, block_terms(): jax.ops.segment_sum(taken_terms, taken_rows, row_blocks)  179 us
    dot_general x3, matrix products, block_terms(): jnp.einsum('nab,nak->nbk', taken, blocked[taken_cols], preferred_element_...  43.1 us
    gather x3, local copies, waits for them, and re-layouts, block_terms(): blocked[taken_cols]  39.8 us
    all_to_all x2, blocking collectives, local(): lax.all_to_all(current.reshape(devices, sub_rows, feature_width), ('row',...  31.5 us
    scatter x1, local copies, waits for them, and re-layouts, local(): outgoing = jnp.zeros((devices, CAP, tile_size, tile_size), jnp.bfloat16)....  30.8 us
  transfers between devices with their start and end apart: 10, of which 8 were waited for; matrix products, arithmetic and copies ran while one was open for 14% of the time, Pallas kernels for 0%

commit v1 on v0

--- a/solution.py
+++ b/solution.py
@@ -86,7 +86,15 @@
         local_gram = jnp.dot(
             scaled.T, scaled, precision=lax.Precision.HIGHEST, preferred_element_type=jnp.float32
         )
-        gram = lax.psum(local_gram, ("row", "col")) / nodes
+
+        def produce_sections(vector):
+            which_axis = "row"
+            device_axis = "col"
+            for dev_j in (device_axis, which_axis):
+                vector = lax.psum(vector, dev_j)
+            return vector
+
+        gram = produce_sections(local_gram) / nodes
         lower = jnp.linalg.cholesky(gram)
         final_output = lax.linalg.triangular_solve(
             lower, scaled, left_side=False, lower=True, transpose_a=True

time: 1210 us -> 1310 us (1.083)
  blocking collectives: 230 us -> 319 us
    psum x3 -> x6, blocking collectives: 199 us -> 284 us  [produce_sections(): vector = lax.psum(vector, dev_j)]
  transfers between devices with their start and end apart: 10 -> 10, of which waited for: 8 -> 8; matrix products, arithmetic and copies ran while one was open for 14% -> 13% of each run, Pallas kernels for 0% -> 0%
where the time goes in v1:
time: 1310 us; the launch traced here: 1290 us
  waiting for transfers between devices  452 us (35%)
  blocking collectives  319 us (24%)
  other arithmetic  283 us (22%)
  local copies, waits for them, and re-layouts  137 us (10%)
  matrix products  59.8 us (5%)
  starting transfers between devices  26.2 us (2%)
  between operations  16.4 us (1%)
    psum x6, blocking collectives, produce_sections(): vector = lax.psum(vector, dev_j)  284 us
    reduce_scatter x3, waiting for transfers between devices, local(): lax.psum_scatter(partial_value.reshape(row_blocks * tile_size, feature_wi...  235 us
    all_gather x3, waiting for transfers between devices, local(): lax.all_gather(received_terms.reshape(rows_dev, feature_width), 'row', ax...  200 us
    scatter-add x3, other arithmetic, block_terms(): jax.ops.segment_sum(taken_terms, taken_rows, row_blocks)  179 us
    dot_general x3, matrix products, block_terms(): jnp.einsum('nab,nak->nbk', taken, blocked[taken_cols], preferred_element_...  43.1 us
    gather x3, local copies, waits for them, and re-layouts, block_terms(): blocked[taken_cols]  39.8 us
    all_to_all x2, blocking collectives, local(): lax.all_to_all(current.reshape(devices, sub_rows, feature_width), ('row',...  35.2 us
    scatter x1, local copies, waits for them, and re-layouts, local(): outgoing = jnp.zeros((devices, CAP, tile_size, tile_size), jnp.bfloat16)....  30.8 us
  transfers between devices with their start and end apart: 10, of which 8 were waited for; matrix products, arithmetic and copies ran while one was open for 13% of the time, Pallas kernels for 0%

profile of v1, /device:TPU:1, one launch (start us, length us, event | category | flops | bytes accessed | tf_op | source)
XLA Modules:
  0.0 1293.3 jit_solution(9744508381227670489)
XLA Ops:
  8.4 10.1 scatter_fusion.1
  20.0 11.5 all-to-all-start.1
  53.4 30.8 %scatter_fusion.2 = bf16[128,3,128,128]{3,2,1,0:T(8,128)(2,1)} fusion(bf16[128,3,128,128]{3,2,1,0:T(8,128)(2,1)} %broadcast_in_dim.14, s32[192]{0:T(256)S(1)} %bitcast.91, bf16[192,128,128]{2,1,0:T(8,128)(2,1)} %param.14), kind=kCustom, calls=%fused_computation.8 | custom fusion | bytes 18875904 | tf_op jit(solution)/shard_map/scatter | solution.py:38
  84.2 10.2 all-to-all-start.2
  97.6 142.3 %all-gather.4.cloned.1.call-done = bf16[16384,64]{1,0:T(8,128)(2,1)} async-done(((bf16[2048,64]{1,0:T(8,128)(2,1)}), bf16[16384,64]{1,0:T(8,128)(2,1)}) %all-gather.4.cloned.1.call-update) | async-done | bytes 2097168 | tf_op jit(solution)/shard_map/all_gather | solution.py:72
  243.8 13.3 %gather_fusion.1 = bf16[384,128,64]{1,2,0:T(8,128)(2,1)} fusion(bf16[128,128,64]{1,2,0:T(8,128)(2,1)S(1)} %copy.77, s32[1024]{0:T(1024)S(1)} %pad_clamp_fusion), kind=kCustom, calls=%fused_computation.1 | custom fusion | bytes 12584448 | tf_op jit(solution)/shard_map/gather | solution.py:15
  265.2 9.0 scatter_fusion
  274.2 9.2 convert_reduce_fusion
  286.7 14.3 %fusion.38 = f32[384,128,64]{1,2,0:T(8,128)} fusion(bf16[384,128,64]{1,2,0:T(8,128)(2,1)} %gather_fusion.1, bf16[384,128,128]{2,1,0:T(8,128)(2,1)} %bitcast.9), kind=kOutput, calls=%fused_computation.120 | convolution fusion | flops 805306368 | bytes 31457280 | tf_op jit(solution)/shard_map/nab,nak->nbk/dot_general | solution.py:14
  305.3 59.8 %scatter_fusion.3 = f32[256,128,64]{1,2,0:T(8,128)} fusion(f32[256,128,64]{1,2,0:T(8,128)} %broadcast.110.clone.3, s32[384]{0:T(512)S(1)} %get-tuple-element.8, f32[384,128,64]{1,2,0:T(8,128)} %fusion.38), kind=kCustom, calls=%fused_computation.9 | custom fusion | flops 3145728 | bytes 37750272 | tf_op jit(solution)/shard_map/scatter-add | solution.py:17
  365.1 8.6 copy_bitcast_fusion.2
  384.0 84.0 %reduce-scatter.4.cloned.1.call-done = bf16[2048,64]{0,1:T(8,128)(2,1)} async-done(((bf16[32768,64]{0,1:T(8,128)(2,1)}), bf16[2048,64]{0,1:T(8,128)(2,1)}) %reduce-scatter.4.cloned.1.call-update) | async-done | bytes 262160 | tf_op jit(solution)/shard_map/reduce_scatter | solution.py:79
  469.7 57.9 %psum.42 = f32[64,64]{0,1:T(8,128)S(1)} all-reduce(f32[64,64]{0,1:T(8,128)S(1)} %fusion.5), channel_id=1, replica_groups=mesh['row'=8,'col'=16] {'col'}, use_global_device_ids=true, to_apply=%region_11.12 | all-reduce | flops 4096 | bytes 32768 | tf_op jit(solution)/shard_map/psum | solution.py:94
  527.6 36.7 %psum.43 = f32[64,64]{0,1:T(8,128)S(1)} all-reduce(f32[64,64]{0,1:T(8,128)S(1)} %psum.42), channel_id=1, replica_groups=mesh['row'=8,'col'=16] {'row'}, use_global_device_ids=true, to_apply=%region_12.13 | all-reduce | flops 4096 | bytes 32768 | tf_op jit(solution)/shard_map/psum | solution.py:94
  578.6 17.6 %all_to_all.25 = bf16[128,2,512]{2,1,0:T(2,128)(2,1)S(1)} all-to-all(bf16[128,2,512]{2,1,0:T(2,128)(2,1)S(1)} %reshape.237), channel_id=1, replica_groups=mesh['row'=8,'col'=16] {'row','col'}, dimensions={0} | all-to-all | bytes 524288 | tf_op jit(solution)/shard_map/all_to_all | solution.py:65
  597.4 28.8 %all-gather.6.cloned.1.call-done = bf16[16384,64]{1,0:T(8,128)(2,1)} async-done(((bf16[2048,64]{1,0:T(8,128)(2,1)}), bf16[16384,64]{1,0:T(8,128)(2,1)}) %all-gather.6.cloned.1.call-update) | async-done | bytes 2097168 | tf_op jit(solution)/shard_map/all_gather | solution.py:72
  630.1 13.3 %gather_fusion.3 = bf16[384,128,64]{1,2,0:T(8,128)(2,1)} fusion(bf16[128,128,64]{1,2,0:T(8,128)(2,1)S(1)} %copy.87, s32[1024]{0:T(1024)S(1)} %pad_clamp_fusion), kind=kCustom, calls=%fused_computation.3 | custom fusion | bytes 12584448 | tf_op jit(solution)/shard_map/gather | solution.py:15
  644.1 14.4 %fusion.39 = f32[384,128,64]{1,2,0:T(8,128)} fusion(bf16[384,128,64]{1,2,0:T(8,128)(2,1)} %gather_fusion.3, bf16[384,128,128]{2,1,0:T(8,128)(2,1)} %bitcast.9), kind=kOutput, calls=%fused_computation.121 | convolution fusion | flops 805306368 | bytes 31457280 | tf_op jit(solution)/shard_map/nab,nak->nbk/dot_general | solution.py:14
  664.4 59.8 %scatter_fusion.5 = f32[256,128,64]{1,2,0:T(8,128)} fusion(f32[256,128,64]{1,2,0:T(8,128)} %broadcast.110.clone.4, s32[384]{0:T(512)S(1)} %get-tuple-element.8, f32[384,128,64]{1,2,0:T(8,128)} %fusion.39), kind=kCustom, calls=%fused_computation.13 | custom fusion | flops 3145728 | bytes 37750272 | tf_op jit(solution)/shard_map/scatter-add | solution.py:17
  728.4 9.2 scatter_fusion.4
  746.3 76.0 %reduce-scatter.6.cloned.1.call-done = bf16[2048,64]{0,1:T(8,128)(2,1)} async-done(((bf16[32768,64]{0,1:T(8,128)(2,1)}), bf16[2048,64]{0,1:T(8,128)(2,1)}) %reduce-scatter.6.cloned.1.call-update) | async-done | bytes 262160 | tf_op jit(solution)/shard_map/reduce_scatter | solution.py:79
  823.9 57.9 %psum.44 = f32[64,64]{0,1:T(8,128)S(1)} all-reduce(f32[64,64]{0,1:T(8,128)S(1)} %fusion.6), channel_id=1, replica_groups=mesh['row'=8,'col'=16] {'col'}, use_global_device_ids=true, to_apply=%region_18.21 | all-reduce | flops 4096 | bytes 32768 | tf_op jit(solution)/shard_map/psum | solution.py:94
  881.8 36.6 %psum.45 = f32[64,64]{0,1:T(8,128)S(1)} all-reduce(f32[64,64]{0,1:T(8,128)S(1)} %psum.44), channel_id=1, replica_groups=mesh['row'=8,'col'=16] {'row'}, use_global_device_ids=true, to_apply=%region_19.22 | all-reduce | flops 4096 | bytes 32768 | tf_op jit(solution)/shard_map/psum | solution.py:94
  932.7 17.6 %all_to_all.26 = bf16[128,2,512]{2,1,0:T(2,128)(2,1)S(1)} all-to-all(bf16[128,2,512]{2,1,0:T(2,128)(2,1)S(1)} %reshape.239), channel_id=1, replica_groups=mesh['row'=8,'col'=16] {'row','col'}, dimensions={0} | all-to-all | bytes 524288 | tf_op jit(solution)/shard_map/all_to_all | solution.py:65
  951.6 28.8 %all-gather.8.cloned.1.call-done = bf16[16384,64]{1,0:T(8,128)(2,1)} async-done(((bf16[2048,64]{1,0:T(8,128)(2,1)}), bf16[16384,64]{1,0:T(8,128)(2,1)}) %all-gather.8.cloned.1.call-update) | async-done | bytes 2097168 | tf_op jit(solution)/shard_map/all_gather | solution.py:72
  984.1 13.3 %gather_fusion.5 = bf16[384,128,64]{1,2,0:T(8,128)(2,1)} fusion(bf16[128,128,64]{1,2,0:T(8,128)(2,1)S(1)} %copy.94, s32[1024]{0:T(1024)S(1)} %pad_clamp_fusion), kind=kCustom, calls=%fused_computation.5 | custom fusion | bytes 12584448 | tf_op jit(solution)/shard_map/gather | solution.py:15
  998.1 14.4 %fusion.40 = f32[384,128,64]{1,2,0:T(8,128)} fusion(bf16[384,128,64]{1,2,0:T(8,128)(2,1)} %gather_fusion.5, bf16[384,128,128]{2,1,0:T(8,128)(2,1)} %bitcast.9), kind=kOutput, calls=%fused_computation.122 | convolution fusion | flops 805306368 | bytes 31457280 | tf_op jit(solution)/shard_map/nab,nak->nbk/dot_general | solution.py:14
  1018.4 58.9 %scatter_fusion.7 = f32[256,128,64]{1,2,0:T(8,128)} fusion(f32[256,128,64]{1,2,0:T(8,128)} %broadcast.110.clone.5, s32[384]{0:T(512)S(1)} %get-tuple-element.8, f32[384,128,64]{1,2,0:T(8,128)} %fusion.40), kind=kCustom, calls=%fused_computation.15 | custom fusion | flops 3145728 | bytes 37750272 | tf_op jit(solution)/shard_map/scatter-add | solution.py:17
  1081.6 9.2 scatter_fusion.6
  1099.4 75.4 %reduce-scatter.8.cloned.1.call-done = bf16[2048,64]{0,1:T(8,128)(2,1)} async-done(((bf16[32768,64]{0,1:T(8,128)(2,1)}), bf16[2048,64]{0,1:T(8,128)(2,1)}) %reduce-scatter.8.cloned.1.call-update) | async-done | bytes 262160 | tf_op jit(solution)/shard_map/reduce_scatter | solution.py:79
  1176.4 57.9 %psum.46 = f32[64,64]{0,1:T(8,128)S(1)} all-reduce(f32[64,64]{0,1:T(8,128)S(1)} %fusion.7), channel_id=1, replica_groups=mesh['row'=8,'col'=16] {'col'}, use_global_device_ids=true, to_apply=%region_23.26 | all-reduce | flops 4096 | bytes 32768 | tf_op jit(solution)/shard_map/psum | solution.py:94
  1234.3 36.6 %psum.47 = f32[64,64]{0,1:T(8,128)S(1)} all-reduce(f32[64,64]{0,1:T(8,128)S(1)} %psum.46), channel_id=1, replica_groups=mesh['row'=8,'col'=16] {'row'}, use_global_device_ids=true, to_apply=%region_24.27 | all-reduce | flops 4096 | bytes 32768 | tf_op jit(solution)/shard_map/psum | solution.py:94
  (109 shorter events, 153.5 us)
Async XLA Ops:
  20.0 21.6 %all-to-all-start.1 = ((s32[128,3,2]{1,2,0:T(2,128)}), s32[128,3,2]{1,2,0:T(2,128)S(1)}, u32[]{:S(2)}, u32[]{:S(2)}) async-start(s32[128,3,2]{1,2,0:T(2,128)} %copy.79), calls=%async_computation.1 | async-start | bytes 262144 | tf_op jit(solution)/shard_map/all_to_all | solution.py:44
  41.6 42.6 %all-to-all-start = ((bf16[128,2,512]{2,1,0:T(2,128)(2,1)}), bf16[128,2,512]{2,1,0:T(2,128)(2,1)S(1)}, u32[]{:S(2)}, u32[]{:S(2)}) async-start(bf16[128,2,512]{2,1,0:T(2,128)(2,1)} %reshape.235), calls=%async_computation | async-start | bytes 524288 | tf_op jit(solution)/shard_map/all_to_all | solution.py:65
  84.2 11.5 copy-start.3
  84.2 11.6 copy-start
  84.2 13.1 %copy-start.4 = (s32[64]{0:T(128)S(1)}, s32[64]{0:T(128)}, u32[]{:S(2)}) copy-start(s32[64]{0:T(128)} %param.13) | copy-start | bytes 772
  84.2 190.0 %all-to-all-start.2 = ((bf16[128,3,128,128]{3,2,1,0:T(8,128)(2,1)}), bf16[128,3,128,128]{3,2,1,0:T(8,128)(2,1)}, u32[]{:S(2)}, u32[]{:S(2)}) async-start(bf16[128,3,128,128]{3,2,1,0:T(8,128)(2,1)} %scatter_fusion.2), calls=%async_computation.2 | async-start | bytes 25165824 | tf_op jit(solution)/shard_map/all_to_all | solution.py:43
  94.5 145.4 %all-gather.4.cloned.1.call-start = ((), (), s32[]{:S(2)}) async-start(), calls=%async_computation.8 | async-start | bytes 4718592 | tf_op jit(solution)/shard_map/all_gather | solution.py:72
  95.7 287.6 %all-reduce.3.cloned.1.call-start = ((), (), s32[]{:S(2)}) async-start(), calls=%async_computation.14 | async-start | bytes 131072
  286.7 181.4 %reduce-scatter.4.cloned.1.call-start = ((), (), s32[]{:S(2)}) async-start(), calls=%async_computation.9 | async-start | bytes 4456448 | tf_op jit(solution)/shard_map/reduce_scatter | solution.py:79
  365.1 8.7 copy-start.5
  373.7 252.5 %all-gather.6.cloned.1.call-start = ((), (), s32[]{:S(2)}) async-start(), calls=%async_computation.10 | async-start | bytes 4718592 | tf_op jit(solution)/shard_map/all_gather | solution.py:72
  597.4 224.9 %reduce-scatter.6.cloned.1.call-start = ((), (), s32[]{:S(2)}) async-start(), calls=%async_computation.11 | async-start | bytes 4456448 | tf_op jit(solution)/shard_map/reduce_scatter | solution.py:79
  644.1 14.4 %copy-start.1 = (bf16[64,128,128]{2,1,0:T(8,128)(2,1)S(1)}, bf16[64,128,128]{2,1,0:T(8,128)(2,1)}, u32[]{:S(2)}) copy-start(bf16[64,128,128]{2,1,0:T(8,128)(2,1)} %param.11) | copy-start | bytes 6291460
  746.2 234.1 %all-gather.8.cloned.1.call-start = ((), (), s32[]{:S(2)}) async-start(), calls=%async_computation.12 | async-start | bytes 4718592 | tf_op jit(solution)/shard_map/all_gather | solution.py:72
  951.5 223.2 %reduce-scatter.8.cloned.1.call-start = ((), (), s32[]{:S(2)}) async-start(), calls=%async_computation.13 | async-start | bytes 4456448 | tf_op jit(solution)/shard_map/reduce_scatter | solution.py:79
  998.1 14.4 %copy-start.2 = (bf16[64,128,128]{2,1,0:T(8,128)(2,1)S(1)}, bf16[64,128,128]{2,1,0:T(8,128)(2,1)}, u32[]{:S(2)}) copy-start(bf16[64,128,128]{2,1,0:T(8,128)(2,1)} %param.11) | copy-start | bytes 6291460
Sparse Core Ops, SparseCore 0:
  97.1 142.6 all-gather.3
  597.5 28.7 all-gather.5
  951.6 28.7 all-gather.7
Sparse Core Ops, SparseCore 1:
  286.7 96.5 all-reduce.2
  386.9 81.1 reduce-scatter.3
  746.3 75.9 reduce-scatter.5
  1099.4 75.3 reduce-scatter.7
